TPU v7x, 768 devices: a whole 4x8x12 slice. The times are simulated.
768 devices in a mesh: dp: 192 (over z, y, core), expert: 4 (over x).
Axes of the slice: x: 4, y: 8, z: 12, core: 2. Of those that a mesh axis runs over, the one named last changes fastest.
Arguments:
- tokens: bfloat16 [98304, 2048], P(('dp', 'expert')), may hold values from -6 to 6
- expert_ids: int32 [98304, 2], P(('dp', 'expert')), may hold values from 0 to 3, all different within a row; in each aligned block of 128 rows (0 to 127, 128 to 255, ...) at most 66 rows name the same one
- gate_probs: bfloat16 [98304, 2], P(('dp', 'expert')), may hold values from 0.099609375 to 1
- w_gate: bfloat16 [4, 2048, 768], P('expert'), may hold values from -0.125 to 0.125
- w_up: bfloat16 [4, 2048, 768], P('expert'), may hold values from -0.125 to 0.125
- w_down: bfloat16 [4, 768, 2048], P('expert'), may hold values from -0.21875 to 0.21875
- teacher_queries: bfloat16 [4, 192, 2048], P('expert', 'dp'), may hold values from -6 to 6
- teacher_passages: bfloat16 [4, 384, 2048], P('expert', 'dp'), may hold values from -6 to 6
- positives: int32 [4, 192], P('expert', 'dp'), may hold values from 0 to 383
Outputs:
- moe_out: bfloat16 [98304, 2048], P(('dp', 'expert'))
- token_grad: bfloat16 [98304, 2048], P(('dp', 'expert'))
- gate_grad: float32 [98304, 2], P(('dp', 'expert'))
- query_loss: float32 [4, 192], P('expert', 'dp')
Inputs may be any that keep to these rules, and one draw needn't show every extreme that they name: `expert_ids`: each token names 2 different experts of its group; among the 128 tokens of one device no expert is named more than 66 times, a bound that some block reaches.
All inputs are finite; a program needn't handle non-finite values.
Results may differ from a plain program's by a relative error of at most 0.015.
Values may be sent and summed in bfloat16 or wider, within the bound.
No kernel may reach another device: no remote copies, remote signals or barrier semaphores. Data moves between devices by JAX's collectives and lax.ppermute only.
A program may use at most 64 MiB of HBM per device.

v0:
```python
import jax
import jax.numpy as jnp
from jax import lax
from jax.sharding import PartitionSpec as P

QLEN = 32
PLEN = 48


student_scale = 50.0
teacher_scale = 80.0
loss_scale = 64.0
norm_eps = 1e-06


def silu_slope(pre_gate):
    sigmoid = jax.nn.sigmoid(pre_gate)
    return sigmoid * (1.0 + pre_gate * (1.0 - sigmoid))


def contract_lead(left_mat, right_mat):
    return lax.dot_general(
        left_mat, right_mat, (((0,), (0,)), ((), ())), preferred_element_type=jnp.float32
    )


def contract_last(left_mat, right_mat):
    return lax.dot_general(
        left_mat, right_mat, (((1,), (1,)), ((), ())), preferred_element_type=jnp.float32
    )


def unit_rows(values):
    as_float = values.astype(jnp.float32)
    inverse = lax.rsqrt(jnp.sum(as_float * as_float, axis=-1, keepdims=True) + norm_eps)
    return (as_float * inverse, inverse)


def unit_back(normed, inverse, grad_normed):
    return inverse * (grad_normed - normed * jnp.sum(normed * grad_normed, axis=-1, keepdims=True))


def shards(
    tokens,
    expert_ids,
    gate_probs,
    w_gate,
    w_up,
    w_down,
    teacher_queries,
    teacher_passages,
    positives,
):
    group_size = lax.axis_size("expert")
    tok_rows, model_width = tokens.shape
    top_count = expert_ids.shape[1]
    query_count = teacher_queries.shape[1]
    local_count = teacher_passages.shape[1]
    capacity = min(tok_rows, (tok_rows * top_count * 33 + 32 * group_size - 1) // (32 * group_size))
    slot_total = group_size * capacity
    flat_ids = expert_ids.reshape(-1)
    row_count = flat_ids.shape[0]
    expert_hits = (flat_ids[:, None] == jnp.arange(group_size, dtype=jnp.int32)[None, :]).astype(
        jnp.int32
    )
    earlier = jnp.cumsum(expert_hits, axis=0) - expert_hits
    slot_index = flat_ids * capacity + jnp.sum(earlier * expert_hits, axis=1)
    slot_source = (
        jnp.full((slot_total,), row_count, jnp.int32)
        .at[slot_index]
        .set(jnp.arange(row_count, dtype=jnp.int32))
    )
    padded_tokens = jnp.concatenate([tokens, jnp.zeros((1, model_width), tokens.dtype)], axis=0)
    send_rows = padded_tokens[slot_source // top_count].reshape(group_size, capacity, model_width)
    gate_flat = gate_probs.reshape(-1, 1).astype(jnp.float32)
    gate_mat = w_gate[0]
    up_mat = w_up[0]
    down_mat = w_down[0]
    arrived = lax.all_to_all(send_rows, "expert", split_axis=0, concat_axis=0, tiled=True)
    sources = arrived.shape[0]
    slot_count = arrived.shape[1]
    arrived_rows = arrived.reshape(-1, model_width)
    pre_gate = jnp.dot(arrived_rows, gate_mat, preferred_element_type=jnp.float32)
    pre_up = jnp.dot(arrived_rows, up_mat, preferred_element_type=jnp.float32)
    hidden = (jax.nn.silu(pre_gate) * pre_up).astype(jnp.bfloat16)
    expert_out = jnp.dot(hidden, down_mat, preferred_element_type=jnp.float32).astype(jnp.bfloat16)
    returned = lax.all_to_all(
        expert_out.reshape(sources, slot_count, model_width),
        "expert",
        split_axis=0,
        concat_axis=0,
        tiled=True,
    )
    saved_gate = pre_gate.reshape(sources, slot_count, -1)
    saved_up = pre_up.reshape(sources, slot_count, -1)
    token_out = returned.reshape(slot_total, model_width)[slot_index].astype(jnp.float32)
    moe_out = jnp.sum(
        (gate_flat * token_out).reshape(tok_rows, top_count, model_width), axis=1
    ).astype(jnp.bfloat16)
    moe_wide = moe_out.astype(jnp.float32)
    query_span = query_count * QLEN
    pooled_q = jnp.mean(moe_wide[:query_span].reshape(query_count, QLEN, model_width), axis=1)
    pooled_p = jnp.mean(moe_wide[query_span:].reshape(local_count, PLEN, model_width), axis=1)
    query_unit, query_inv = unit_rows(pooled_q)
    passage_unit, passage_inv = unit_rows(pooled_p)
    query_half = query_unit.astype(jnp.bfloat16)
    passage_half = passage_unit.astype(jnp.bfloat16)
    teacher_q_half = unit_rows(teacher_queries[0])[0].astype(jnp.bfloat16)
    teacher_p_half = unit_rows(teacher_passages[0])[0].astype(jnp.bfloat16)
    dp_count = lax.axis_size("dp")
    total_count = local_count * dp_count
    student_part = student_scale * contract_last(
        query_half, lax.all_gather(passage_half, "dp", axis=0, tiled=True)
    )
    teacher_part = teacher_scale * contract_last(
        teacher_q_half, lax.all_gather(teacher_p_half, "dp", axis=0, tiled=True)
    )
    student_exp = jnp.exp(student_part)
    teacher_exp = jnp.exp(teacher_part)
    student_total = jnp.sum(student_exp, axis=1)
    teacher_total = jnp.sum(teacher_exp, axis=1)
    cross_term = jnp.sum(teacher_exp * (teacher_part - student_part), axis=1)
    is_positive = positives[0][:, None] == jnp.arange(total_count, dtype=jnp.int32)[None, :]
    positive_score = jnp.sum(jnp.where(is_positive, student_part, 0.0), axis=1)
    query_loss = (
        2.0 * jnp.log(student_total)
        - positive_score
        + cross_term / teacher_total
        - jnp.log(teacher_total)
    )
    coeffs = (
        2.0 * student_exp / student_total[:, None]
        - teacher_exp / teacher_total[:, None]
        - is_positive.astype(jnp.float32)
    ).astype(jnp.bfloat16)
    columns = coeffs
    unit_q_grad = student_scale * jnp.dot(
        columns,
        lax.all_gather(passage_half, "dp", axis=0, tiled=True),
        preferred_element_type=jnp.float32,
    )
    columns = coeffs
    unit_p_grad = lax.psum_scatter(
        student_scale * contract_lead(columns, query_half), "dp", scatter_dimension=0, tiled=True
    )
    query_grad = unit_back(query_unit, query_inv, unit_q_grad)
    passage_grad = unit_back(passage_unit, passage_inv, unit_p_grad)
    out_grad = jnp.concatenate(
        [
            jnp.repeat(query_grad * (loss_scale / QLEN), QLEN, axis=0),
            jnp.repeat(passage_grad * (loss_scale / PLEN), PLEN, axis=0),
        ],
        axis=0,
    )
    grad_rep = jnp.repeat(out_grad, top_count, axis=0)
    routed_grad = (gate_flat * grad_rep).astype(jnp.bfloat16)
    padded_grad = jnp.concatenate([routed_grad, jnp.zeros((1, model_width), jnp.bfloat16)], axis=0)
    send_grads = padded_grad[slot_source].reshape(group_size, capacity, model_width)
    arrived_grad = lax.all_to_all(send_grads, "expert", split_axis=0, concat_axis=0, tiled=True)
    grad_rows = arrived_grad.reshape(-1, model_width)
    pre_gate = saved_gate.reshape(grad_rows.shape[0], -1)
    pre_up = saved_up.reshape(grad_rows.shape[0], -1)
    hidden_grad = contract_last(grad_rows, down_mat)
    gate_part = (hidden_grad * pre_up * silu_slope(pre_gate)).astype(jnp.bfloat16)
    up_part = (hidden_grad * jax.nn.silu(pre_gate)).astype(jnp.bfloat16)
    row_grad = (contract_last(gate_part, gate_mat) + contract_last(up_part, up_mat)).astype(
        jnp.bfloat16
    )
    back_grad = lax.all_to_all(
        row_grad.reshape(group_size, capacity, model_width),
        "expert",
        split_axis=0,
        concat_axis=0,
        tiled=True,
    )
    token_row_grad = back_grad.reshape(slot_total, model_width)[slot_index].astype(jnp.float32)
    token_grad = jnp.sum(token_row_grad.reshape(tok_rows, top_count, model_width), axis=1).astype(
        jnp.bfloat16
    )
    gate_grad = jnp.sum(token_out * grad_rep, axis=1).reshape(tok_rows, top_count)
    return (moe_out, token_grad, gate_grad, query_loss[None])


def solution(mesh):
    in_specs = (
        P(("dp", "expert"), None),
        P(("dp", "expert"), None),
        P(("dp", "expert"), None),
        P("expert", None, None),
        P("expert", None, None),
        P("expert", None, None),
        P("expert", "dp", None),
        P("expert", "dp", None),
        P("expert", "dp"),
    )
    out_specs = (
        P(("dp", "expert"), None),
        P(("dp", "expert"), None),
        P(("dp", "expert"), None),
        P("expert", "dp"),
    )
    return jax.shard_map(shards, mesh=mesh, in_specs=in_specs, out_specs=out_specs, check_vma=False)
```

profile of v0, /device:TPU:1, one launch (start us, length us, event | category | flops | bytes accessed | tf_op | source)
XLA Modules:
  0.0 681.6 jit_solution(12241933445715440679)
XLA Ops:
  14.5 6.0 gather_fusion
  20.5 2.6 reshape.259
  23.0 5.0 all-to-all-start
  28.8 9.7 %all-to-all-done = bf16[4,66,2048]{2,1,0:T(8,128)(2,1)} async-done(((bf16[4,66,2048]{2,1,0:T(8,128)(2,1)}), bf16[4,66,2048]{2,1,0:T(8,128)(2,1)}, u32[]{:S(2)}, u32[]{:S(2)}) %all-to-all-start) | async-done | bytes 1081376 | tf_op jit(solution)/shard_map/all_to_all | solution.py:79
  38.5 2.5 reshape.260
  41.1 3.4 fusion.10
  48.6 2.6 reshape.261
  51.1 4.4 all-to-all-start.1
  55.9 10.1 %all-to-all-done.1 = bf16[4,66,2048]{2,1,0:T(8,128)(2,1)} async-done(((bf16[4,66,2048]{2,1,0:T(8,128)(2,1)}), bf16[4,66,2048]{2,1,0:T(8,128)(2,1)}, u32[]{:S(2)}, u32[]{:S(2)}) %all-to-all-start.1) | async-done | bytes 1081376 | tf_op jit(solution)/shard_map/all_to_all | solution.py:87
  66.0 2.5 reshape.262
  68.6 4.8 gather_fusion.1
  73.4 3.4 reshape.271
  76.8 4.8 multiply_reduce_fusion.1
  90.1 61.9 %all-gather.7.cloned.1.call-done = bf16[192,2,2048]{2,1,0:T(2,128)(2,1)} async-done(((bf16[1,2,2048]{2,1,0:T(2,128)(2,1)}), bf16[192,2,2048]{2,1,0:T(2,128)(2,1)}) %all-gather.7.cloned.1.call-update) | async-done | bytes 1572880 | tf_op jit(solution)/shard_map/all_gather | solution.py:116
  152.0 3.7 reshape.321
  157.6 107.0 %all-gather.5.cloned.1.call-done = bf16[192,2,2048]{2,1,0:T(2,128)(2,1)} async-done(((bf16[1,2,2048]{2,1,0:T(2,128)(2,1)}), bf16[192,2,2048]{2,1,0:T(2,128)(2,1)}) %all-gather.5.cloned.1.call-update) | async-done | bytes 1572880 | tf_op jit(solution)/shard_map/all_gather | solution.py:113
  264.6 3.6 reshape.319
  279.1 309.0 %all-reduce.5.cloned.1.call-done = f32[384,2048]{1,0:T(8,128)} async-done(((f32[384,2048]{1,0:T(8,128)}), f32[384,2048]{1,0:T(8,128)}) %all-reduce.5.cloned.1.call-update) | async-done | bytes 3145744
  590.3 2.5 broadcast_in_dim.19
  592.8 3.7 reshape.266
  599.8 6.2 gather_fusion.2
  606.0 2.5 reshape.267
  608.5 20.0 %all_to_all.20 = bf16[4,66,2048]{2,1,0:T(8,128)(2,1)} all-to-all(bf16[4,66,2048]{2,1,0:T(8,128)(2,1)} %reshape.267), channel_id=1, replica_groups=mesh['dp'=192,'expert'=4] {'expert'}, dimensions={0} | all-to-all | bytes 2162688 | tf_op jit(solution)/shard_map/all_to_all | solution.py:159
  628.5 2.6 reshape.268
  631.1 2.4 fusion
  637.8 2.6 reshape.269
  640.4 4.5 all-to-all-start.3
  648.8 10.6 %all-to-all-done.3 = bf16[4,66,2048]{2,1,0:T(8,128)(2,1)} async-done(((bf16[4,66,2048]{2,1,0:T(8,128)(2,1)}), bf16[4,66,2048]{2,1,0:T(8,128)(2,1)}, u32[]{:S(2)}, u32[]{:S(2)}) %all-to-all-start.3) | async-done | bytes 1081376 | tf_op jit(solution)/shard_map/all_to_all | solution.py:169
  659.5 2.6 reshape.270
  662.1 4.7 gather_fusion.3
  666.8 2.5 gather.18
  669.3 4.6 reduce_sum.164
  (93 shorter events, 41.4 us)
Async XLA Ops:
  7.2 39.3 %copy-start = (bf16[1,768,2048]{2,1,0:T(8,128)(2,1)S(1)}, bf16[1,768,2048]{2,1,0:T(8,128)(2,1)}, u32[]{:S(2)}) copy-start(bf16[1,768,2048]{2,1,0:T(8,128)(2,1)} %param.14) | copy-start | bytes 9437188
  23.0 5.0 copy-start.4
  23.0 15.5 %all-to-all-start = ((bf16[4,66,2048]{2,1,0:T(8,128)(2,1)}), bf16[4,66,2048]{2,1,0:T(8,128)(2,1)}, u32[]{:S(2)}, u32[]{:S(2)}) async-start(bf16[4,66,2048]{2,1,0:T(8,128)(2,1)} %reshape.259), calls=%async_computation | async-start | bytes 2359296 | tf_op jit(solution)/shard_map/all_to_all | solution.py:79
  28.0 124.0 %all-gather.7.cloned.1.call-start = ((), (), s32[]{:S(2)}) async-start(), calls=%async_computation.5 | async-start | bytes 1581056 | tf_op jit(solution)/shard_map/all_gather | solution.py:116
  41.1 3.4 copy-start.2
  41.1 3.5 copy-start.6
  44.6 1.0 copy-start.9
  45.6 0.9 copy-start.11
  51.1 4.6 copy-start.5
  51.1 14.9 %all-to-all-start.1 = ((bf16[4,66,2048]{2,1,0:T(8,128)(2,1)}), bf16[4,66,2048]{2,1,0:T(8,128)(2,1)}, u32[]{:S(2)}, u32[]{:S(2)}) async-start(bf16[4,66,2048]{2,1,0:T(8,128)(2,1)} %reshape.261), calls=%async_computation.1 | async-start | bytes 2359296 | tf_op jit(solution)/shard_map/all_to_all | solution.py:87
  55.5 209.1 %all-gather.5.cloned.1.call-start = ((), (), s32[]{:S(2)}) async-start(), calls=%async_computation.4 | async-start | bytes 1581056 | tf_op jit(solution)/shard_map/all_gather | solution.py:113
  81.6 0.8 copy-start.1
  82.4 3.9 copy-start.3
  85.4 502.8 %all-reduce.5.cloned.1.call-start = ((), (), s32[]{:S(2)}) async-start(), calls=%async_computation.6 | async-start | bytes 6291456
  631.1 2.5 copy-start.7
  631.1 2.5 copy-start.10
  633.5 1.9 copy-start.8
  633.5 2.1 copy-start.12
  640.4 19.1 %all-to-all-start.3 = ((bf16[4,66,2048]{2,1,0:T(8,128)(2,1)}), bf16[4,66,2048]{2,1,0:T(8,128)(2,1)}, u32[]{:S(2)}, u32[]{:S(2)}) async-start(bf16[4,66,2048]{2,1,0:T(8,128)(2,1)} %reshape.269), calls=%async_computation.3 | async-start | bytes 2359296 | tf_op jit(solution)/shard_map/all_to_all | solution.py:169
Sparse Core Ops, SparseCore 0:
  33.1 118.8 all-gather.6
  155.8 108.8 all-gather.4
  274.2 313.9 all-reduce.4
where the time goes:
time: 685 us; the launch traced here: 682 us
  waiting for transfers between devices  508 us (74%)
  local copies, waits for them, and re-layouts  73.9 us (11%)
  other arithmetic  26.1 us (4%)
  between operations  21.1 us (3%)
  blocking collectives  20 us (3%)
  matrix products  17.7 us (3%)
  starting transfers between devices  14.4 us (2%)
    unnamed x4, waiting for transfers between devices  309 us
    all_gather x1, waiting for transfers between devices, shards(): lax.all_gather(passage_half, 'dp', axis=0, tiled=True)  107 us
    all_gather x1, waiting for transfers between devices, shards(): lax.all_gather(teacher_p_half, 'dp', axis=0, tiled=True)  61.9 us
    all_to_all x1, blocking collectives, shards(): lax.all_to_all(send_grads, 'expert', split_axis=0, concat_axis=0, tiled=T...  20 us
  transfers between devices with their start and end apart: 6, of which 6 were waited for; matrix products, arithmetic and copies ran while one was open for 6% of the time, Pallas kernels for 0%

commit v1 on v0

v1 whole, which is shorter than its diff:
```python
import functools

import jax
import jax.numpy as jnp
import numpy as np
from jax import lax
from jax.experimental import pallas as pl
from jax.experimental.pallas import tpu as pltpu
from jax.sharding import Mesh
from jax.sharding import PartitionSpec as P

QLEN = 32
PLEN = 48
SEGS = 3
CHUNKS = 8
Z_CHIPS = 12

student_scale = 50.0
teacher_scale = 80.0
loss_scale = 64.0
norm_eps = 1e-06

f32 = jnp.float32
bf16 = jnp.bfloat16
exact = lax.Precision.HIGHEST


def iota(shape, axis):
    return lax.broadcasted_iota(jnp.int32, shape, axis)


def dot(left, right, dims=((1,), (0,)), precision=None):
    return lax.dot_general(left, right, (dims, ((), ())), precision=precision, preferred_element_type=f32)


def silu_slope(pre_gate):
    sigmoid = jax.nn.sigmoid(pre_gate)
    return sigmoid * (1.0 + pre_gate * (1.0 - sigmoid))


def segment_mask(rows, count, repeat):
    token = iota((rows, count), 1)
    text = jnp.where(token < QLEN, 0, jnp.where(token < QLEN + PLEN, 1, 2))
    return (text == iota((rows, count), 0) // repeat).astype(f32)


def routing(ids):
    count = ids.shape[1]
    expert = iota((8, count), 0)
    first = expert == ids[0:1, :]
    second = expert == ids[1:2, :]
    hit = jnp.where(first, 1.0, jnp.where(second, 1.0, 0.0))
    before = (iota((count, count), 0) < iota((count, count), 1)).astype(bf16)
    rank = dot(hit.astype(bf16), before)
    return jnp.where(hit > 0.0, rank, -1.0), first, second


def slot_hits(rank, experts, rows):
    count = rank.shape[1]
    slot = iota((rows, count), 0).astype(f32)
    return [(slot == rank[e : e + 1, :]).astype(f32) for e in range(experts)]


def dispatch_kernel(tok_ref, ids_ref, prob_ref, send_ref, *, experts, cap, rows):
    count = tok_ref.shape[0]
    rank, first, second = routing(ids_ref[...])
    probs = prob_ref[...].astype(f32)
    weight = jnp.where(first, probs[0:1, :], jnp.where(second, probs[1:2, :], 0.0))
    wide = slot_hits(rank, experts, 128)
    segs = segment_mask(8, count, 1)
    place = (iota((rows, 8), 0) == cap + iota((rows, 8), 1)).astype(bf16)
    metas = []
    for e in range(experts):
        by_text = (segs * weight[e : e + 1, :]).astype(bf16)
        meta = dot(by_text, wide[e].astype(bf16), ((1,), (1,)))
        metas.append(dot(place, meta.astype(bf16)))
    pick = jnp.concatenate([hits[:rows] for hits in wide], axis=0).astype(bf16)
    width = tok_ref.shape[1]
    send_ref[:, 0:128] = (dot(pick, tok_ref[:, 0:128]) + jnp.concatenate(metas, axis=0)).astype(bf16)
    send_ref[:, 128:width] = dot(pick, tok_ref[:, 128:width]).astype(bf16)


def unit_block(values):
    inverse = lax.rsqrt(jnp.sum(values * values, keepdims=True) + norm_eps)
    return values * inverse, inverse


def to_chunks(row, size):
    which = iota((CHUNKS, size), 0)
    out = jnp.zeros((CHUNKS, size), f32)
    for j in range(CHUNKS):
        out = jnp.where(which == j, row[:, j * size : (j + 1) * size], out)
    return out


def combine_kernel(
    ret_ref, ids_ref, prob_ref, tq_ref, tp_ref, pos_ref, moe_ref, unit_ref, inv_ref, qs_ref, ps_ref, *, experts, rows
):
    count = ids_ref.shape[1]
    width = ret_ref.shape[1]
    size = width // CHUNKS
    rank, first, second = routing(ids_ref[...])
    probs = prob_ref[...].astype(f32)
    weight = jnp.where(first, probs[0:1, :], jnp.where(second, probs[1:2, :], 0.0))
    hits = slot_hits(rank, experts, rows)
    mix = jnp.concatenate([hits[e] * weight[e : e + 1, :] for e in range(experts)], axis=0).astype(bf16)
    moe = dot(mix, ret_ref[...], ((0,), (0,))).astype(bf16)
    moe_ref[...] = moe
    member = segment_mask(SEGS * CHUNKS, count, CHUNKS).astype(bf16)
    chunk = iota((SEGS * CHUNKS, size), 0) % CHUNKS
    pooled = jnp.zeros((SEGS * CHUNKS, size), f32)
    for j in range(CHUNKS):
        pooled = jnp.where(chunk == j, dot(member, moe[:, j * size : (j + 1) * size]), pooled)
    query, query_inv = unit_block(pooled[0:8] * (1.0 / QLEN))
    pass_a, pass_a_inv = unit_block(pooled[8:16] * (1.0 / PLEN))
    pass_b, pass_b_inv = unit_block(pooled[16:24] * (1.0 / PLEN))
    unit_ref[...] = jnp.concatenate([query, pass_a, pass_b], axis=0)
    inv_ref[...] = jnp.concatenate(
        [jnp.broadcast_to(inverse, (8, 128)) for inverse in (query_inv, pass_a_inv, pass_b_inv)], axis=0
    )
    teach_q = unit_block(to_chunks(tq_ref[...].astype(f32), size))[0]
    teach_p = tp_ref[...].astype(f32)
    teach_a = unit_block(to_chunks(teach_p[0:1], size))[0]
    teach_b = unit_block(to_chunks(teach_p[1:2], size))[0]
    pos = pos_ref[0, 0]
    lane = iota((8, size), 1)
    marks = jnp.where(lane == 0, (pos >> 4).astype(f32), jnp.where(lane == 1, (pos & 15).astype(f32), 0.0))
    queries = jnp.concatenate([query, teach_q, marks], axis=0).astype(bf16)
    passages = jnp.concatenate([pass_a, pass_b, teach_a, teach_b], axis=0).astype(bf16)
    for peer in range(qs_ref.shape[0]):
        qs_ref[peer] = queries
    for peer in range(ps_ref.shape[0]):
        ps_ref[peer] = passages


def passage_of(col):
    return (col // 32) * 2 + (col % 16) // 8


def score_kernel(q_ref, p_ref, me_ref, sums_ref, saved_ref, *, peers):
    q_rows = q_ref.shape[0]
    p_rows = p_ref.shape[0]
    valid_count = p_rows // 16
    queries = q_ref[...]
    products = dot(queries, p_ref[...], ((1,), (1,)))
    row = iota((q_rows, p_rows), 0)
    col = iota((q_rows, p_rows), 1)
    kind = row % 24 // 8
    wanted = jnp.where(col % 32 < 16, 0, 1)
    products = jnp.where((kind == wanted) & (row % 8 == col % 8), products, 0.0)
    pick_row = iota((2 * peers, q_rows), 0)
    pick_col = iota((2 * peers, q_rows), 1)
    pick = ((pick_col // 24 == pick_row % peers) & (pick_col % 24 // 8 == pick_row // peers)).astype(f32)
    join = (passage_of(iota((p_rows, 128), 0)) == iota((p_rows, 128), 1)).astype(f32)
    scores = dot(dot(pick, products, precision=exact), join, precision=exact)
    student = student_scale * scores[0:peers]
    teacher = teacher_scale * scores[peers : 2 * peers]
    mark_pick = (iota((peers, q_rows), 1) == 24 * iota((peers, q_rows), 0) + 16).astype(bf16)
    marks = dot(mark_pick, queries)
    pos = (16.0 * marks[:, 0:1] + marks[:, 1:2]).astype(jnp.int32)
    lane = iota((peers, 128), 1)
    me = me_ref[0, 0]
    number = (lane // 2) * (2 * peers) + lane % 2 + 2 * me
    valid = lane < valid_count
    is_pos = jnp.where(valid & (number == pos), 1.0, 0.0)
    student_exp = jnp.where(valid, jnp.exp(student), 0.0)
    teacher_exp = jnp.where(valid, jnp.exp(teacher), 0.0)
    total = lambda values: jnp.sum(values, axis=1, keepdims=True)
    sums = jnp.where(
        lane == 0,
        total(student_exp),
        jnp.where(
            lane == 1,
            total(teacher_exp),
            jnp.where(
                lane == 2, total(teacher_exp * (teacher - student)), jnp.where(lane == 3, total(is_pos * student), 0.0)
            ),
        ),
    )
    for peer in range(peers):
        sums_ref[peer] = sums
    saved_ref[0] = student_exp
    saved_ref[1] = teacher_exp
    saved_ref[2] = is_pos


def coeff_kernel(sums_ref, saved_ref, q_ref, p_ref, me_ref, dq_ref, dp_ref, loss_ref, *, peers):
    q_rows = q_ref.shape[0]
    p_rows = p_ref.shape[0]
    sums = sums_ref[0]
    for peer in range(1, peers):
        sums = sums + sums_ref[peer]
    student_total = sums[:, 0:1]
    teacher_total = sums[:, 1:2]
    loss = 2.0 * jnp.log(student_total) - sums[:, 3:4] + sums[:, 2:3] / teacher_total - jnp.log(teacher_total)
    mine = iota((peers, 128), 0) == me_ref[0, 0]
    loss_ref[...] = jnp.sum(jnp.where(mine, loss, 0.0), axis=0, keepdims=True)
    coeffs = (2.0 * saved_ref[0] / student_total - saved_ref[1] / teacher_total - saved_ref[2]).astype(bf16)
    rows = peers * CHUNKS
    spread = (iota((rows, peers), 0) // CHUNKS == iota((rows, peers), 1)).astype(bf16)
    join = (iota((128, p_rows), 0) == passage_of(iota((128, p_rows), 1))).astype(bf16)
    by_query = dot(dot(spread, coeffs).astype(bf16), join)
    row = iota((rows, p_rows), 0)
    col = iota((rows, p_rows), 1)
    by_query = jnp.where((col % 32 < 16) & (row % 8 == col % 8), by_query, 0.0).astype(bf16)
    dq_ref[...] = student_scale * dot(by_query, p_ref[...])
    rows = p_rows // 2
    spread = (iota((rows, 128), 0) // CHUNKS == iota((rows, 128), 1)).astype(bf16)
    join = (iota((peers, q_rows), 0) == iota((peers, q_rows), 1) // 24).astype(bf16)
    by_passage = dot(dot(spread, coeffs, ((1,), (1,))).astype(bf16), join)
    row = iota((rows, q_rows), 0)
    col = iota((rows, q_rows), 1)
    by_passage = jnp.where((col % 24 < 8) & (row % 8 == col % 8), by_passage, 0.0).astype(bf16)
    dp_ref[...] = student_scale * dot(by_passage, q_ref[...])


def grad_kernel(dq_ref, dp_ref, unit_ref, inv_ref, grad_ref, sent_ref):
    query = dq_ref[0]
    for peer in range(1, dq_ref.shape[0]):
        query = query + dq_ref[peer]
    passage = dp_ref[0]
    for peer in range(1, dp_ref.shape[0]):
        passage = passage + dp_ref[peer]
    parts = []
    for s, (unit_grad, scale) in enumerate(
        ((query, loss_scale / QLEN), (passage[0:8], loss_scale / PLEN), (passage[8:16], loss_scale / PLEN))
    ):
        unit = unit_ref[8 * s : 8 * s + 8, :]
        inverse = inv_ref[8 * s : 8 * s + 8, 0:1]
        along = jnp.sum(unit * unit_grad, keepdims=True)
        parts.append(scale * (inverse * (unit_grad - unit * along)))
    grad = jnp.concatenate(parts, axis=0)
    grad_ref[...] = grad
    for peer in range(sent_ref.shape[0]):
        sent_ref[peer] = grad


def gate_grad_kernel(ret_ref, ids_ref, grad_ref, out_ref, *, experts, rows):
    count = ids_ref.shape[1]
    size = ret_ref.shape[1] // CHUNKS
    slots = ret_ref.shape[0]
    rank, first, second = routing(ids_ref[...])
    grad = grad_ref[...]
    high = grad.astype(bf16)
    low = (grad - high.astype(f32)).astype(bf16)
    both = jnp.concatenate([high.astype(f32), low.astype(f32)], axis=0).astype(bf16)
    n = 2 * SEGS * CHUNKS
    chunk = iota((n, slots), 0) % CHUNKS
    acc = jnp.zeros((n, slots), f32)
    for j in range(CHUNKS):
        part = dot(both, ret_ref[:, j * size : (j + 1) * size], ((1,), (1,)))
        acc = jnp.where(chunk == j, part, acc)
    gather = (iota((8, n), 1) // CHUNKS % SEGS == iota((8, n), 0)).astype(f32)
    by_slot = dot(gather, acc, precision=exact)
    hits = slot_hits(rank, experts, rows)
    texts = segment_mask(8, count, 1)
    results = []
    for named in (first, second):
        named = jnp.where(named, 1.0, 0.0)
        pick = jnp.concatenate([hits[e] * named[e : e + 1, :] for e in range(experts)], axis=0)
        results.append(jnp.sum(texts * dot(by_slot, pick, precision=exact), axis=0, keepdims=True))
    out_ref[...] = jnp.where(iota((2, count), 0) == 0, results[0], results[1])


def token_grad_kernel(back_ref, ids_ref, out_ref, *, experts, rows):
    rank, _, _ = routing(ids_ref[...])
    pick = jnp.concatenate(slot_hits(rank, experts, rows), axis=0).astype(bf16)
    out_ref[...] = dot(pick, back_ref[...], ((0,), (0,))).astype(bf16)


def vmem(count):
    return [pl.BlockSpec(memory_space=pltpu.VMEM)] * count


SMEM = pl.BlockSpec(memory_space=pltpu.SMEM)


def shape_of(*dims, dtype=f32):
    return jax.ShapeDtypeStruct(dims, dtype)


def exchange(values, axis):
    return lax.all_to_all(values, axis, split_axis=0, concat_axis=0, tiled=True)


def shards(
    tokens,
    expert_ids,
    gate_probs,
    w_gate,
    w_up,
    w_down,
    teacher_queries,
    teacher_passages,
    positives,
):
    experts = lax.axis_size("expert")
    peers = lax.axis_size("yc")
    chips = lax.axis_size("z")
    count, width = tokens.shape
    size = width // CHUNKS
    top = expert_ids.shape[1]
    cap = min(count, (count * top * 33 + 32 * experts - 1) // (32 * experts))
    rows = (cap + SEGS + 7) // 8 * 8
    slots = experts * rows
    ids = expert_ids.T
    probs = gate_probs.T
    me = lax.axis_index("yc").astype(jnp.int32).reshape(1, 1)
    gate_mat = w_gate[0]
    up_mat = w_up[0]
    down_mat = w_down[0]

    sent = pl.pallas_call(
        functools.partial(dispatch_kernel, experts=experts, cap=cap, rows=rows),
        out_shape=shape_of(slots, width, dtype=bf16),
        in_specs=vmem(3),
        out_specs=vmem(1)[0],
        name="dispatch",
    )(tokens, ids, probs)
    arrived = exchange(sent.reshape(experts, rows, width), "expert")
    arrived_rows = arrived.reshape(slots, width)
    pre_gate = jnp.dot(arrived_rows, gate_mat, preferred_element_type=f32)
    pre_up = jnp.dot(arrived_rows, up_mat, preferred_element_type=f32)
    hidden = (jax.nn.silu(pre_gate) * pre_up).astype(bf16)
    expert_out = jnp.dot(hidden, down_mat, preferred_element_type=f32).astype(bf16)
    returned = exchange(expert_out.reshape(experts, rows, width), "expert").reshape(slots, width)

    moe_out, unit, inverse, q_sent, p_sent = pl.pallas_call(
        functools.partial(combine_kernel, experts=experts, rows=rows),
        out_shape=(
            shape_of(count, width, dtype=bf16),
            shape_of(SEGS * CHUNKS, size),
            shape_of(SEGS * CHUNKS, 128),
            shape_of(peers, 24, size, dtype=bf16),
            shape_of(chips, 32, size, dtype=bf16),
        ),
        in_specs=vmem(5) + [SMEM],
        out_specs=tuple(vmem(5)),
        name="combine",
    )(returned, ids, probs, teacher_queries[0], teacher_passages[0], positives)
    q_all = exchange(q_sent, "yc").reshape(peers * 24, size)
    p_all = exchange(p_sent, "z").reshape(chips * 32, size)
    sums_sent, saved = pl.pallas_call(
        functools.partial(score_kernel, peers=peers),
        out_shape=(shape_of(peers, peers, 128), shape_of(3, peers, 128)),
        in_specs=vmem(2) + [SMEM],
        out_specs=tuple(vmem(2)),
        name="score",
    )(q_all, p_all, me)
    sums = exchange(sums_sent, "yc")
    dq_sent, dp_sent, loss = pl.pallas_call(
        functools.partial(coeff_kernel, peers=peers),
        out_shape=(shape_of(peers * CHUNKS, size), shape_of(chips * 16, size), shape_of(1, 128)),
        in_specs=vmem(4) + [SMEM],
        out_specs=tuple(vmem(3)),
        name="coeff",
    )(sums, saved, q_all, p_all, me)
    dq = exchange(dq_sent.reshape(peers, CHUNKS, size), "yc")
    dp = exchange(dp_sent.reshape(chips, 2 * CHUNKS, size), "z")
    grad, grad_sent = pl.pallas_call(
        grad_kernel,
        out_shape=(shape_of(SEGS * CHUNKS, size), shape_of(experts, SEGS * CHUNKS, size)),
        in_specs=vmem(4),
        out_specs=tuple(vmem(2)),
        name="text_grad",
    )(dq, dp, unit, inverse)
    grad_all = exchange(grad_sent, "expert").reshape(experts * SEGS, width)

    grad_high = grad_all.astype(bf16)
    grad_low = (grad_all - grad_high.astype(f32)).astype(bf16)
    text_hidden = lax.dot_general(
        jnp.concatenate([grad_high, grad_low], axis=0),
        down_mat,
        (((1,), (1,)), ((), ())),
        preferred_element_type=f32,
    )
    text_hidden = (text_hidden[: experts * SEGS] + text_hidden[experts * SEGS :]).reshape(experts, SEGS, -1)
    share = arrived[:, cap : cap + SEGS, :rows].astype(f32)
    hidden_grad = sum(share[:, s, :, None] * text_hidden[:, s, None, :] for s in range(SEGS)).reshape(slots, -1)
    gate_part = (hidden_grad * pre_up * silu_slope(pre_gate)).astype(bf16)
    up_part = (hidden_grad * jax.nn.silu(pre_gate)).astype(bf16)
    row_grad = (
        dot(gate_part, gate_mat, ((1,), (1,))) + dot(up_part, up_mat, ((1,), (1,)))
    ).astype(bf16)
    back = exchange(row_grad.reshape(experts, rows, width), "expert").reshape(slots, width)
    gate_grad = pl.pallas_call(
        functools.partial(gate_grad_kernel, experts=experts, rows=rows),
        out_shape=shape_of(top, count),
        in_specs=vmem(3),
        out_specs=vmem(1)[0],
        name="gate_grad",
    )(returned, ids, grad)
    token_grad = pl.pallas_call(
        functools.partial(token_grad_kernel, experts=experts, rows=rows),
        out_shape=shape_of(count, width, dtype=bf16),
        in_specs=vmem(2),
        out_specs=vmem(1)[0],
        name="token_grad",
    )(back, ids)
    return (moe_out, token_grad, gate_grad.T, loss[:, :1])


def solution(mesh):
    dp, expert = mesh.devices.shape
    chips = Z_CHIPS if dp % Z_CHIPS == 0 else 2
    grid = Mesh(np.asarray(mesh.devices).reshape(chips, dp // chips, expert), ("z", "yc", "expert"))
    every = ("z", "yc", "expert")
    in_specs = (
        P(every, None),
        P(every, None),
        P(every, None),
        P("expert", None, None),
        P("expert", None, None),
        P("expert", None, None),
        P("expert", ("z", "yc"), None),
        P("expert", ("z", "yc"), None),
        P("expert", ("z", "yc")),
    )
    out_specs = (
        P(every, None),
        P(every, None),
        P(every, None),
        P("expert", ("z", "yc")),
    )
    return jax.shard_map(shards, mesh=grid, in_specs=in_specs, out_specs=out_specs, check_vma=False)
```

time: 685 us -> 196 us (0.29)
  the two profiles are of different devices: /device:TPU:1 before, /device:TPU:64 now
where the time goes in v1:
time: 196 us; the launch traced here: 195 us
  blocking collectives  63.6 us (32%)
  waiting for transfers between devices  61.9 us (32%)
  starting transfers between devices  30.7 us (16%)
  Pallas kernels  19.1 us (10%)
  matrix products  10.4 us (5%)
  local copies, waits for them, and re-layouts  4.84 us (2%)
  other arithmetic  2.73 us (1%)
    all_to_all x4, blocking collectives, exchange(): return lax.all_to_all(values, axis, split_axis=0, concat_axis=0, tiled=True)  63.6 us
    all_to_all x5, waiting for transfers between devices, exchange(): return lax.all_to_all(values, axis, split_axis=0, concat_axis=0, tiled=True)  61.9 us
    all_to_all x5, starting transfers between devices, exchange(): return lax.all_to_all(values, axis, split_axis=0, concat_axis=0, tiled=True)  30.7 us
    unnamed x20, local copies, waits for them, and re-layouts  4.49 us
  transfers between devices with their start and end apart: 5, of which 5 were waited for; matrix products, arithmetic and copies ran while one was open for 1% of the time, Pallas kernels for 1%

profile of v1, /device:TPU:64, one launch (start us, length us, event | category | flops | bytes accessed | tf_op | source)
XLA Modules:
  0.0 194.7 jit_solution(16297978970232599170)
XLA Ops:
  0.6 3.5 %dispatch.1 = bf16[288,2048]{1,0:T(8,128)(2,1)} custom-call(bf16[128,2048]{1,0:T(8,128)(2,1)} %tok_ref.1, s32[2,128]{1,0:T(2,128)} %bitcast.105, bf16[2,128]{1,0:T(2,128)(2,1)} %bitcast.111), custom_call_target="tpu_custom_call" | custom-call | tf_op jit(solution)/shard_map/dispatch/pallas_call | solution.py:313
  4.1 20.8 %all_to_all.45 = bf16[4,72,2048]{2,1,0:T(8,128)(2,1)S(1)} all-to-all(bf16[4,72,2048]{2,1,0:T(8,128)(2,1)} %bitcast.93), channel_id=1, replica_groups=mesh['z'=12,'yc'=16,'expert'=4] {'expert'}, dimensions={0} | all-to-all | bytes 2359296 | tf_op jit(solution)/shard_map/all_to_all | solution.py:283
  24.9 1.1 fusion.6
  26.0 1.2 copy-done.7
  27.2 1.1 fusion.10
  28.3 1.1 copy-done.1
  29.4 2.2 %fusion.18 = bf16[288,2048]{1,0:T(8,128)(2,1)} fusion(bf16[1,768,2048]{2,1,0:T(8,128)(2,1)S(1)} %copy-done.1, f32[288,768]{1,0:T(8,128)S(1)} %fusion.6, f32[288,768]{1,0:T(8,128)S(1)} %fusion.10), kind=kOutput, calls=%fused_computation.14 | convolution fusion | flops 907886592 | bytes 6094848 | tf_op jit(solution)/shard_map/dot_general | solution.py:325
  31.6 4.3 %all-to-all-start.1 = ((bf16[4,72,2048]{2,1,0:T(8,128)(2,1)}), bf16[4,72,2048]{2,1,0:T(8,128)(2,1)}, u32[]{:S(2)}, u32[]{:S(2)}) async-start(bf16[4,72,2048]{2,1,0:T(8,128)(2,1)} %bitcast.101), calls=%async_computation.1 | async-start | bytes 2359296 | tf_op jit(solution)/shard_map/all_to_all | solution.py:283
  36.5 15.1 %all-to-all-done.1 = bf16[4,72,2048]{2,1,0:T(8,128)(2,1)} async-done(((bf16[4,72,2048]{2,1,0:T(8,128)(2,1)}), bf16[4,72,2048]{2,1,0:T(8,128)(2,1)}, u32[]{:S(2)}, u32[]{:S(2)}) %all-to-all-start.1) | async-done | bytes 1179680 | tf_op jit(solution)/shard_map/all_to_all | solution.py:283
  51.6 2.9 %combine.1 = (bf16[128,2048]{1,0:T(8,128)(2,1)}, f32[24,256]{1,0:T(8,128)}, f32[24,128]{1,0:T(8,128)}, bf16[16,24,256]{2,1,0:T(8,128)(2,1)}, bf16[12,32,256]{2,1,0:T(8,128)(2,1)}) custom-call(bf16[288,2048]{1,0:T(8,128)(2,1)} %bitcast.8.ret_ref, s32[2,128]{1,0:T(2,128)} %bitcast.106, bf16[2,128]{1,0:T(2,128)(2,1)} %bitcast.112, bf16[1,2048]{1,0:T(2,128)(2,1)} %bitcast.109, ...), custom_call_target="tpu_custom_call" | custom-call | tf_op jit(solution)/shard_map/combine/pallas_call | solution.py:328
  54.5 17.2 %all_to_all.46 = bf16[16,24,256]{2,1,0:T(8,128)(2,1)} all-to-all(bf16[16,24,256]{2,1,0:T(8,128)(2,1)} %get-tuple-element.17), channel_id=1, replica_groups=mesh['z'=12,'yc'=16,'expert'=4] {'yc'}, dimensions={0} | all-to-all | bytes 393216 | tf_op jit(solution)/shard_map/all_to_all | solution.py:283
  71.7 14.8 %all-to-all-start.3 = ((bf16[12,32,256]{2,1,0:T(8,128)(2,1)}), bf16[12,32,256]{2,1,0:T(8,128)(2,1)S(1)}, u32[]{:S(2)}, u32[]{:S(2)}) async-start(bf16[12,32,256]{2,1,0:T(8,128)(2,1)} %get-tuple-element.18), calls=%async_computation.3 | async-start | bytes 393216 | tf_op jit(solution)/shard_map/all_to_all | solution.py:283
  86.5 14.4 %all-to-all-done.3 = bf16[12,32,256]{2,1,0:T(8,128)(2,1)S(1)} async-done(((bf16[12,32,256]{2,1,0:T(8,128)(2,1)}), bf16[12,32,256]{2,1,0:T(8,128)(2,1)S(1)}, u32[]{:S(2)}, u32[]{:S(2)}) %all-to-all-start.3) | async-done | bytes 196640 | tf_op jit(solution)/shard_map/all_to_all | solution.py:283
  101.6 3.0 %score.1 = (f32[16,16,128]{2,1,0:T(8,128)}, f32[3,16,128]{2,1,0:T(8,128)}) custom-call(bf16[384,256]{1,0:T(8,128)(2,1)} %bitcast.94, bf16[384,256]{1,0:T(8,128)(2,1)} %bitcast.96, s32[1,1]{1,0:T(1,128)} %bitcast.13.me_ref), custom_call_target="tpu_custom_call" | custom-call | tf_op jit(solution)/shard_map/score/pallas_call | solution.py:343
  104.6 12.8 %all_to_all.47.sums_ref = f32[16,16,128]{2,1,0:T(8,128)} all-to-all(f32[16,16,128]{2,1,0:T(8,128)} %get-tuple-element.19), channel_id=1, replica_groups=mesh['z'=12,'yc'=16,'expert'=4] {'yc'}, dimensions={0} | all-to-all | bytes 262144 | tf_op jit(solution)/shard_map/all_to_all | solution.py:283
  117.4 2.5 %coeff.1 = (f32[128,256]{1,0:T(8,128)}, f32[192,256]{1,0:T(8,128)}, f32[1,128]{1,0:T(1,128)}) custom-call(f32[16,16,128]{2,1,0:T(8,128)} %all_to_all.47.sums_ref, f32[3,16,128]{2,1,0:T(8,128)} %get-tuple-element.20.saved_ref, bf16[384,256]{1,0:T(8,128)(2,1)} %bitcast.95, bf16[384,256]{1,0:T(8,128)(2,1)} %bitcast.97, s32[1,1]{1,0:T(1,128)} %bitcast.13.me_ref), custom_call_target="tpu_custom_call" | custom-call | tf_op jit(solution)/shard_map/coeff/pallas_call | solution.py:351
  119.9 12.8 %all_to_all.48.dq_ref = f32[16,8,256]{2,1,0:T(8,128)} all-to-all(f32[16,8,256]{2,1,0:T(8,128)} %bitcast.103), channel_id=1, replica_groups=mesh['z'=12,'yc'=16,'expert'=4] {'yc'}, dimensions={0} | all-to-all | bytes 262144 | tf_op jit(solution)/shard_map/all_to_all | solution.py:283
  132.7 4.1 %all-to-all-start.6 = ((f32[12,16,256]{2,1,0:T(8,128)}), f32[12,16,256]{2,1,0:T(8,128)S(1)}, u32[]{:S(2)}, u32[]{:S(2)}) async-start(f32[12,16,256]{2,1,0:T(8,128)} %bitcast.102), calls=%async_computation.6 | async-start | bytes 393216 | tf_op jit(solution)/shard_map/all_to_all | solution.py:283
  136.7 0.7 slice_convert_fusion
  137.4 13.9 %all-to-all-done.6.dp_ref = f32[12,16,256]{2,1,0:T(8,128)S(1)} async-done(((f32[12,16,256]{2,1,0:T(8,128)}), f32[12,16,256]{2,1,0:T(8,128)S(1)}, u32[]{:S(2)}, u32[]{:S(2)}) %all-to-all-start.6) | async-done | bytes 196640 | tf_op jit(solution)/shard_map/all_to_all | solution.py:283
  152.0 1.8 text_grad.1
  153.8 3.3 %all-to-all-start.7 = ((f32[4,24,256]{2,1,0:T(8,128)}), f32[4,24,256]{2,1,0:T(8,128)S(1)}, u32[]{:S(2)}, u32[]{:S(2)}) async-start(f32[4,24,256]{2,1,0:T(8,128)} %get-tuple-element.25), calls=%async_computation.7 | async-start | bytes 196608 | tf_op jit(solution)/shard_map/all_to_all | solution.py:283
  157.4 5.5 %all-to-all-done.7 = f32[4,24,256]{2,1,0:T(8,128)S(1)} async-done(((f32[4,24,256]{2,1,0:T(8,128)}), f32[4,24,256]{2,1,0:T(8,128)S(1)}, u32[]{:S(2)}, u32[]{:S(2)}) %all-to-all-start.7) | async-done | bytes 98336 | tf_op jit(solution)/shard_map/all_to_all | solution.py:283
  162.9 2.8 %fusion = f32[24,768]{1,0:T(8,128)S(1)} fusion(bf16[1,768,2048]{2,1,0:T(8,128)(2,1)} %param.14, bf16[12,2048]{1,0:T(8,128)(2,1)S(1)} %get-tuple-element.31, bf16[12,2048]{1,0:T(8,128)(2,1)S(1)} %get-tuple-element.32), kind=kOutput, calls=%fused_computation | convolution fusion | flops 75694080 | bytes 3317760 | tf_op jit(solution)/shard_map/dot_general | solution.py:371
  165.9 2.0 %fusion.26 = (bf16[288,768]{1,0:T(8,128)(2,1)S(1)}, bf16[288,768]{1,0:T(8,128)(2,1)S(1)}) fusion(f32[288,768]{1,0:T(8,128)} %copy-done.4, f32[288,768]{1,0:T(8,128)} %copy-done.5, f32[4,768]{1,0:T(4,128)S(1)} %get-tuple-element.38, f32[288]{0:T(512)S(1)} %mul.97, f32[4,768]{1,0:T(4,128)S(1)} %get-tuple-element.39, f32[288]{0:T(512)S(1)} %mul.91, ...), kind=kLoop, calls=%fused_computation.23 | loop fusion | flops 3981312 | bytes 2694528 | tf_op jit(solution)/shard_map/convert_element_type | solution.py:380
  167.9 1.1 fusion.4
  169.0 0.8 copy-done.8
  169.8 2.2 %fusion.15 = bf16[288,2048]{1,0:T(8,128)(2,1)} fusion(f32[288,2048]{1,0:T(8,128)S(1)} %fusion.4, bf16[288,768]{1,0:T(8,128)(2,1)S(1)} %get-tuple-element.33, bf16[1,2048,768]{2,1,0:T(8,128)(2,1)S(1)} %copy-done.8), kind=kOutput, calls=%fused_computation.13 | convolution fusion | flops 907149312 | bytes 7127040 | tf_op jit(solution)/shard_map/dot_general | solution.py:33
  171.9 4.3 %all-to-all-start.8 = ((bf16[4,72,2048]{2,1,0:T(8,128)(2,1)}), bf16[4,72,2048]{2,1,0:T(8,128)(2,1)}, u32[]{:S(2)}, u32[]{:S(2)}) async-start(bf16[4,72,2048]{2,1,0:T(8,128)(2,1)} %bitcast.100), calls=%async_computation.8 | async-start | bytes 2359296 | tf_op jit(solution)/shard_map/all_to_all | solution.py:283
  176.2 2.7 %gate_grad.1 = f32[2,128]{1,0:T(2,128)} custom-call(bf16[288,2048]{1,0:T(8,128)(2,1)} %bitcast.8.ret_ref, s32[2,128]{1,0:T(2,128)} %bitcast.107, f32[24,256]{1,0:T(8,128)} %get-tuple-element.26.grad_ref), custom_call_target="tpu_custom_call" | custom-call | tf_op jit(solution)/shard_map/gate_grad/pallas_call | solution.py:386
  178.9 13.1 %all-to-all-done.8 = bf16[4,72,2048]{2,1,0:T(8,128)(2,1)} async-done(((bf16[4,72,2048]{2,1,0:T(8,128)(2,1)}), bf16[4,72,2048]{2,1,0:T(8,128)(2,1)}, u32[]{:S(2)}, u32[]{:S(2)}) %all-to-all-start.8) | async-done | bytes 1179680 | tf_op jit(solution)/shard_map/all_to_all | solution.py:283
  192.0 2.7 %token_grad.1 = bf16[128,2048]{1,0:T(8,128)(2,1)} custom-call(bf16[288,2048]{1,0:T(8,128)(2,1)} %bitcast.20.back_ref, s32[2,128]{1,0:T(2,128)} %bitcast.108), custom_call_target="tpu_custom_call" | custom-call | tf_op jit(solution)/shard_map/token_grad/pallas_call | solution.py:393
  (26 shorter events, 1.8 us)
Async XLA Ops:
  0.6 24.3 %copy-start = (bf16[1,2048,768]{2,1,0:T(8,128)(2,1)S(1)}, bf16[1,2048,768]{2,1,0:T(8,128)(2,1)}, u32[]{:S(2)}) copy-start(bf16[1,2048,768]{2,1,0:T(8,128)(2,1)} %param.13) | copy-start | bytes 9437188
  24.9 1.1 copy-start.3
  24.9 2.3 %copy-start.7 = (bf16[1,2048,768]{2,1,0:T(8,128)(2,1)S(1)}, bf16[1,2048,768]{2,1,0:T(8,128)(2,1)}, u32[]{:S(2)}) copy-start(bf16[1,2048,768]{2,1,0:T(8,128)(2,1)} %param.12) | copy-start | bytes 9437188
  27.2 4.4 %copy-start.4 = (f32[288,768]{1,0:T(8,128)}, f32[288,768]{1,0:T(8,128)S(1)}, u32[]{:S(2)}) copy-start(f32[288,768]{1,0:T(8,128)S(1)} %fusion.6) | copy-start | bytes 2654212
  27.2 2.2 %copy-start.1 = (bf16[1,768,2048]{2,1,0:T(8,128)(2,1)S(1)}, bf16[1,768,2048]{2,1,0:T(8,128)(2,1)}, u32[]{:S(2)}) copy-start(bf16[1,768,2048]{2,1,0:T(8,128)(2,1)} %param.14) | copy-start | bytes 9437188
  29.4 2.2 %copy-start.5 = (f32[288,768]{1,0:T(8,128)}, f32[288,768]{1,0:T(8,128)S(1)}, u32[]{:S(2)}) copy-start(f32[288,768]{1,0:T(8,128)S(1)} %fusion.10) | copy-start | bytes 2654212
  31.6 20.0 %all-to-all-start.1 = ((bf16[4,72,2048]{2,1,0:T(8,128)(2,1)}), bf16[4,72,2048]{2,1,0:T(8,128)(2,1)}, u32[]{:S(2)}, u32[]{:S(2)}) async-start(bf16[4,72,2048]{2,1,0:T(8,128)(2,1)} %bitcast.101), calls=%async_computation.1 | async-start | bytes 2359296 | tf_op jit(solution)/shard_map/all_to_all | solution.py:283
  71.7 29.2 %all-to-all-start.3 = ((bf16[12,32,256]{2,1,0:T(8,128)(2,1)}), bf16[12,32,256]{2,1,0:T(8,128)(2,1)S(1)}, u32[]{:S(2)}, u32[]{:S(2)}) async-start(bf16[12,32,256]{2,1,0:T(8,128)(2,1)} %get-tuple-element.18), calls=%async_computation.3 | async-start | bytes 393216 | tf_op jit(solution)/shard_map/all_to_all | solution.py:283
  100.9 0.7 copy-start.2
  132.7 18.6 %all-to-all-start.6 = ((f32[12,16,256]{2,1,0:T(8,128)}), f32[12,16,256]{2,1,0:T(8,128)S(1)}, u32[]{:S(2)}, u32[]{:S(2)}) async-start(f32[12,16,256]{2,1,0:T(8,128)} %bitcast.102), calls=%async_computation.6 | async-start | bytes 393216 | tf_op jit(solution)/shard_map/all_to_all | solution.py:283
  151.3 0.7 copy-start.6
  153.8 9.1 %all-to-all-start.7 = ((f32[4,24,256]{2,1,0:T(8,128)}), f32[4,24,256]{2,1,0:T(8,128)S(1)}, u32[]{:S(2)}, u32[]{:S(2)}) async-start(f32[4,24,256]{2,1,0:T(8,128)} %get-tuple-element.25), calls=%async_computation.7 | async-start | bytes 196608 | tf_op jit(solution)/shard_map/all_to_all | solution.py:283
  167.9 1.9 copy-start.8
  171.9 20.1 %all-to-all-start.8 = ((bf16[4,72,2048]{2,1,0:T(8,128)(2,1)}), bf16[4,72,2048]{2,1,0:T(8,128)(2,1)}, u32[]{:S(2)}, u32[]{:S(2)}) async-start(bf16[4,72,2048]{2,1,0:T(8,128)(2,1)} %bitcast.100), calls=%async_computation.8 | async-start | bytes 2359296 | tf_op jit(solution)/shard_map/all_to_all | solution.py:283

commit v2 on v1

--- a/solution.py
+++ b/solution.py
@@ -31,11 +31,6 @@
 
 def dot(left, right, dims=((1,), (0,)), precision=None):
     return lax.dot_general(left, right, (dims, ((), ())), precision=precision, preferred_element_type=f32)
-
-
-def silu_slope(pre_gate):
-    sigmoid = jax.nn.sigmoid(pre_gate)
-    return sigmoid * (1.0 + pre_gate * (1.0 - sigmoid))
 
 
 def segment_mask(rows, count, repeat):
@@ -137,93 +132,103 @@
     return (col // 32) * 2 + (col % 16) // 8
 
 
-def score_kernel(q_ref, p_ref, me_ref, sums_ref, saved_ref, *, peers):
+def score_kernel(q_ref, p_ref, me_ref, sent_ref, saved_ref, *, peers):
     q_rows = q_ref.shape[0]
-    p_rows = p_ref.shape[0]
+    p_rows, size = p_ref.shape
     valid_count = p_rows // 16
     queries = q_ref[...]
-    products = dot(queries, p_ref[...], ((1,), (1,)))
+    passages = p_ref[...]
+    products = dot(queries, passages, ((1,), (1,)))
     row = iota((q_rows, p_rows), 0)
     col = iota((q_rows, p_rows), 1)
-    kind = row % 24 // 8
     wanted = jnp.where(col % 32 < 16, 0, 1)
-    products = jnp.where((kind == wanted) & (row % 8 == col % 8), products, 0.0)
-    pick_row = iota((2 * peers, q_rows), 0)
-    pick_col = iota((2 * peers, q_rows), 1)
-    pick = ((pick_col // 24 == pick_row % peers) & (pick_col % 24 // 8 == pick_row // peers)).astype(f32)
+    products = jnp.where((row % 24 // 8 == wanted) & (row % 8 == col % 8), products, 0.0)
+    products = jnp.sum(products.reshape(3 * peers, 8, p_rows), axis=1)
     join = (passage_of(iota((p_rows, 128), 0)) == iota((p_rows, 128), 1)).astype(f32)
-    scores = dot(dot(pick, products, precision=exact), join, precision=exact)
+    scores = dot(products, join, precision=exact)
+    pick_row = iota((2 * peers, 3 * peers), 0)
+    pick = (iota((2 * peers, 3 * peers), 1) == 3 * (pick_row % peers) + pick_row // peers).astype(f32)
+    scores = dot(pick, scores, precision=exact)
     student = student_scale * scores[0:peers]
     teacher = teacher_scale * scores[peers : 2 * peers]
     mark_pick = (iota((peers, q_rows), 1) == 24 * iota((peers, q_rows), 0) + 16).astype(bf16)
     marks = dot(mark_pick, queries)
     pos = (16.0 * marks[:, 0:1] + marks[:, 1:2]).astype(jnp.int32)
     lane = iota((peers, 128), 1)
-    me = me_ref[0, 0]
-    number = (lane // 2) * (2 * peers) + lane % 2 + 2 * me
+    number = (lane // 2) * (2 * peers) + lane % 2 + 2 * me_ref[0, 0]
     valid = lane < valid_count
     is_pos = jnp.where(valid & (number == pos), 1.0, 0.0)
     student_exp = jnp.where(valid, jnp.exp(student), 0.0)
     teacher_exp = jnp.where(valid, jnp.exp(teacher), 0.0)
-    total = lambda values: jnp.sum(values, axis=1, keepdims=True)
-    sums = jnp.where(
-        lane == 0,
-        total(student_exp),
-        jnp.where(
-            lane == 1,
-            total(teacher_exp),
-            jnp.where(
-                lane == 2, total(teacher_exp * (teacher - student)), jnp.where(lane == 3, total(is_pos * student), 0.0)
-            ),
-        ),
-    )
-    for peer in range(peers):
-        sums_ref[peer] = sums
     saved_ref[0] = student_exp
     saved_ref[1] = teacher_exp
     saved_ref[2] = is_pos
-
-
-def coeff_kernel(sums_ref, saved_ref, q_ref, p_ref, me_ref, dq_ref, dp_ref, loss_ref, *, peers):
+    parts = (student_exp, teacher_exp, teacher_exp * (teacher - student), is_pos * student)
+    sums = jnp.zeros((peers, 128), f32)
+    for n, part in enumerate(parts):
+        rest = jnp.sum(part, axis=1, keepdims=True)
+        for piece in range(3):
+            head = rest.astype(bf16).astype(f32)
+            sums = jnp.where(lane == 4 * piece + n, head, sums)
+            rest = rest - head
+    sums = jnp.concatenate([sums[0 : peers // 2], sums[peers // 2 : peers]], axis=1)
+    if sums.shape[0] < 8:
+        sums = jnp.concatenate([sums] + [jnp.zeros_like(sums)] * (8 // sums.shape[0] - 1), axis=0)
+    sums = sums.astype(bf16)
+    weights = jnp.concatenate([student_exp, teacher_exp, is_pos], axis=0).astype(bf16)
+    row = iota((q_rows, 3 * peers), 0)
+    spread = (iota((q_rows, 3 * peers), 1) == (row % 24 // 8) * peers + row // 24).astype(bf16)
+    join = (iota((128, p_rows), 0) == passage_of(iota((128, p_rows), 1))).astype(bf16)
+    mixing = dot(dot(spread, weights).astype(bf16), join)
+    row = iota((q_rows, p_rows), 0)
+    mixing = jnp.where((col % 32 < 16) & (row % 8 == col % 8), mixing, 0.0).astype(bf16)
+    mixed = dot(mixing, passages)
+    for peer in range(peers):
+        sent_ref[peer, 0:24, :] = mixed[24 * peer : 24 * peer + 24].astype(bf16)
+        sent_ref[peer, 24:32, :] = sums
+
+
+def coeff_kernel(got_ref, saved_ref, q_ref, me_ref, dq_ref, dp_ref, loss_ref, *, peers):
     q_rows = q_ref.shape[0]
-    p_rows = p_ref.shape[0]
-    sums = sums_ref[0]
+    rows = dp_ref.shape[0]
+    total = got_ref[0].astype(f32)
     for peer in range(1, peers):
-        sums = sums + sums_ref[peer]
-    student_total = sums[:, 0:1]
-    teacher_total = sums[:, 1:2]
-    loss = 2.0 * jnp.log(student_total) - sums[:, 3:4] + sums[:, 2:3] / teacher_total - jnp.log(teacher_total)
-    mine = iota((peers, 128), 0) == me_ref[0, 0]
-    loss_ref[...] = jnp.sum(jnp.where(mine, loss, 0.0), axis=0, keepdims=True)
+        total = total + got_ref[peer].astype(f32)
+    half = peers // 2
+
+    def quantity(n):
+        cols = []
+        for side in (0, 128):
+            at = side + n
+            block = total[24 : 24 + half]
+            cols.append(block[:, at : at + 1] + block[:, at + 4 : at + 5] + block[:, at + 8 : at + 9])
+        return jnp.concatenate(cols, axis=0)
+
+    student_total, teacher_total, cross, positive = quantity(0), quantity(1), quantity(2), quantity(3)
+    loss = 2.0 * jnp.log(student_total) - positive + cross / teacher_total - jnp.log(teacher_total)
+    mine = iota((peers, 1), 0) == me_ref[0, 0]
+    own = lambda values: jnp.sum(jnp.where(mine, values, 0.0), keepdims=True)
+    loss_ref[...] = jnp.broadcast_to(own(loss), (1, 128))
+    dq_ref[...] = student_scale * (
+        total[0:8] * (2.0 / own(student_total)) - total[8:16] / own(teacher_total) - total[16:24]
+    )
     coeffs = (2.0 * saved_ref[0] / student_total - saved_ref[1] / teacher_total - saved_ref[2]).astype(bf16)
-    rows = peers * CHUNKS
-    spread = (iota((rows, peers), 0) // CHUNKS == iota((rows, peers), 1)).astype(bf16)
-    join = (iota((128, p_rows), 0) == passage_of(iota((128, p_rows), 1))).astype(bf16)
-    by_query = dot(dot(spread, coeffs).astype(bf16), join)
-    row = iota((rows, p_rows), 0)
-    col = iota((rows, p_rows), 1)
-    by_query = jnp.where((col % 32 < 16) & (row % 8 == col % 8), by_query, 0.0).astype(bf16)
-    dq_ref[...] = student_scale * dot(by_query, p_ref[...])
-    rows = p_rows // 2
     spread = (iota((rows, 128), 0) // CHUNKS == iota((rows, 128), 1)).astype(bf16)
     join = (iota((peers, q_rows), 0) == iota((peers, q_rows), 1) // 24).astype(bf16)
     by_passage = dot(dot(spread, coeffs, ((1,), (1,))).astype(bf16), join)
     row = iota((rows, q_rows), 0)
     col = iota((rows, q_rows), 1)
     by_passage = jnp.where((col % 24 < 8) & (row % 8 == col % 8), by_passage, 0.0).astype(bf16)
-    dp_ref[...] = student_scale * dot(by_passage, q_ref[...])
+    dp_ref[...] = (student_scale * dot(by_passage, q_ref[...])).astype(bf16)
 
 
 def grad_kernel(dq_ref, dp_ref, unit_ref, inv_ref, grad_ref, sent_ref):
-    query = dq_ref[0]
-    for peer in range(1, dq_ref.shape[0]):
-        query = query + dq_ref[peer]
-    passage = dp_ref[0]
+    passage = dp_ref[0].astype(f32)
     for peer in range(1, dp_ref.shape[0]):
-        passage = passage + dp_ref[peer]
+        passage = passage + dp_ref[peer].astype(f32)
     parts = []
     for s, (unit_grad, scale) in enumerate(
-        ((query, loss_scale / QLEN), (passage[0:8], loss_scale / PLEN), (passage[8:16], loss_scale / PLEN))
+        ((dq_ref[...], loss_scale / QLEN), (passage[0:8], loss_scale / PLEN), (passage[8:16], loss_scale / PLEN))
     ):
         unit = unit_ref[8 * s : 8 * s + 8, :]
         inverse = inv_ref[8 * s : 8 * s + 8, 0:1]
@@ -233,6 +238,74 @@
     grad_ref[...] = grad
     for peer in range(sent_ref.shape[0]):
         sent_ref[peer] = grad
+
+
+def forward_kernel(x_ref, gate_ref, up_ref, down_ref, out_ref, pre_gate_ref, pre_up_ref, acc_ref):
+    step = pl.program_id(0)
+    rows = x_ref[...]
+    pre_gate = dot(rows, gate_ref[...])
+    pre_up = dot(rows, up_ref[...])
+    pre_gate_ref[...] = pre_gate
+    pre_up_ref[...] = pre_up
+    hidden = (jax.nn.silu(pre_gate) * pre_up).astype(bf16)
+    part = dot(hidden, down_ref[...])
+
+    @pl.when(step == 0)
+    def _():
+        acc_ref[...] = part
+
+    @pl.when(step > 0)
+    def _():
+        acc_ref[...] += part
+
+    @pl.when(step == pl.num_programs(0) - 1)
+    def _():
+        out_ref[...] = acc_ref[...].astype(bf16)
+
+
+def backward_kernel(
+    grad_ref, share_ref, pre_gate_ref, pre_up_ref, gate_ref, up_ref, down_ref, out_ref, acc_ref, *, experts, rows, at
+):
+    step = pl.program_id(0)
+    grad = grad_ref[...]
+    texts, size = grad.shape
+    block = down_ref.shape[0]
+    high = grad.astype(bf16)
+    low = (grad - high.astype(f32)).astype(bf16)
+    both = jnp.concatenate([high, low], axis=0)
+    chunk = iota((2 * texts, block), 0) % CHUNKS
+    by_text = jnp.zeros((2 * texts, block), f32)
+    for j in range(CHUNKS):
+        part = dot(both, down_ref[:, j * size : (j + 1) * size], ((1,), (1,)))
+        by_text = jnp.where(chunk == j, part, by_text)
+    row = iota((experts * 8, 2 * texts), 0)
+    text = iota((experts * 8, 2 * texts), 1) % texts // CHUNKS
+    pick = ((text // SEGS == row // 8) & (text % SEGS + at == row % 8)).astype(f32)
+    by_text = dot(pick, by_text, precision=exact)
+    hidden_grad = jnp.concatenate(
+        [
+            dot(share_ref[s].astype(f32), by_text[8 * s : 8 * s + 8], ((0,), (0,)), precision=exact)[:rows]
+            for s in range(experts)
+        ],
+        axis=0,
+    )
+    pre_gate = pre_gate_ref[...]
+    sigmoid = jax.nn.sigmoid(pre_gate)
+    gate_part = (hidden_grad * pre_up_ref[...] * (sigmoid * (1.0 + pre_gate * (1.0 - sigmoid)))).astype(bf16)
+    up_part = (hidden_grad * (pre_gate * sigmoid)).astype(bf16)
+    part = dot(gate_part, gate_ref[...], ((1,), (1,))) + dot(up_part, up_ref[...], ((1,), (1,)))
+
+    @pl.when(step == 0)
+    def _():
+        acc_ref[...] = part
+
+    @pl.when(step > 0)
+    def _():
+        acc_ref[...] += part
+
+    @pl.when(step == pl.num_programs(0) - 1)
+    def _():
+        out_ref[...] = acc_ref[...].astype(bf16)
 
 
 def gate_grad_kernel(ret_ref, ids_ref, grad_ref, out_ref, *, experts, rows):
@@ -318,11 +391,25 @@
         name="dispatch",
     )(tokens, ids, probs)
     arrived = exchange(sent.reshape(experts, rows, width), "expert")
-    arrived_rows = arrived.reshape(slots, width)
-    pre_gate = jnp.dot(arrived_rows, gate_mat, preferred_element_type=f32)
-    pre_up = jnp.dot(arrived_rows, up_mat, preferred_element_type=f32)
-    hidden = (jax.nn.silu(pre_gate) * pre_up).astype(bf16)
-    expert_out = jnp.dot(hidden, down_mat, preferred_element_type=f32).astype(bf16)
+    hidden_size = gate_mat.shape[1]
+    block = 256
+    whole = lambda *dims: pl.BlockSpec(dims, lambda i: (0,) * len(dims))
+    wide = pl.BlockSpec((width, block), lambda i: (0, i))
+    tall = pl.BlockSpec((block, width), lambda i: (i, 0))
+    pre = pl.BlockSpec((slots, block), lambda i: (0, i))
+    expert_out, pre_gate, pre_up = pl.pallas_call(
+        forward_kernel,
+        grid=(hidden_size // block,),
+        out_shape=(
+            shape_of(slots, width, dtype=bf16),
+            shape_of(slots, hidden_size),
+            shape_of(slots, hidden_size),
+        ),
+        in_specs=[whole(slots, width), wide, wide, tall],
+        out_specs=(whole(slots, width), pre, pre),
+        scratch_shapes=[pltpu.VMEM((slots, width), f32)],
+        name="expert_forward",
+    )(arrived.reshape(slots, width), gate_mat, up_mat, down_mat)
     returned = exchange(expert_out.reshape(experts, rows, width), "expert").reshape(slots, width)
 
     moe_out, unit, inverse, q_sent, p_sent = pl.pallas_call(
@@ -340,22 +427,21 @@
     )(returned, ids, probs, teacher_queries[0], teacher_passages[0], positives)
     q_all = exchange(q_sent, "yc").reshape(peers * 24, size)
     p_all = exchange(p_sent, "z").reshape(chips * 32, size)
-    sums_sent, saved = pl.pallas_call(
+    mixed_sent, saved = pl.pallas_call(
         functools.partial(score_kernel, peers=peers),
-        out_shape=(shape_of(peers, peers, 128), shape_of(3, peers, 128)),
+        out_shape=(shape_of(peers, 32, size, dtype=bf16), shape_of(3, peers, 128)),
         in_specs=vmem(2) + [SMEM],
         out_specs=tuple(vmem(2)),
         name="score",
     )(q_all, p_all, me)
-    sums = exchange(sums_sent, "yc")
-    dq_sent, dp_sent, loss = pl.pallas_call(
+    mixed = exchange(mixed_sent, "yc")
+    dq, dp_sent, loss = pl.pallas_call(
         functools.partial(coeff_kernel, peers=peers),
-        out_shape=(shape_of(peers * CHUNKS, size), shape_of(chips * 16, size), shape_of(1, 128)),
-        in_specs=vmem(4) + [SMEM],
+        out_shape=(shape_of(CHUNKS, size), shape_of(chips * 16, size, dtype=bf16), shape_of(1, 128)),
+        in_specs=vmem(3) + [SMEM],
         out_specs=tuple(vmem(3)),
         name="coeff",
-    )(sums, saved, q_all, p_all, me)
-    dq = exchange(dq_sent.reshape(peers, CHUNKS, size), "yc")
+    )(mixed, saved, q_all, me)
     dp = exchange(dp_sent.reshape(chips, 2 * CHUNKS, size), "z")
     grad, grad_sent = pl.pallas_call(
         grad_kernel,
@@ -364,24 +450,24 @@
         out_specs=tuple(vmem(2)),
         name="text_grad",
     )(dq, dp, unit, inverse)
-    grad_all = exchange(grad_sent, "expert").reshape(experts * SEGS, width)
-
-    grad_high = grad_all.astype(bf16)
-    grad_low = (grad_all - grad_high.astype(f32)).astype(bf16)
-    text_hidden = lax.dot_general(
-        jnp.concatenate([grad_high, grad_low], axis=0),
-        down_mat,
-        (((1,), (1,)), ((), ())),
-        preferred_element_type=f32,
-    )
-    text_hidden = (text_hidden[: experts * SEGS] + text_hidden[experts * SEGS :]).reshape(experts, SEGS, -1)
-    share = arrived[:, cap : cap + SEGS, :rows].astype(f32)
-    hidden_grad = sum(share[:, s, :, None] * text_hidden[:, s, None, :] for s in range(SEGS)).reshape(slots, -1)
-    gate_part = (hidden_grad * pre_up * silu_slope(pre_gate)).astype(bf16)
-    up_part = (hidden_grad * jax.nn.silu(pre_gate)).astype(bf16)
-    row_grad = (
-        dot(gate_part, gate_mat, ((1,), (1,))) + dot(up_part, up_mat, ((1,), (1,)))
-    ).astype(bf16)
+    grad_all = exchange(grad_sent, "expert").reshape(experts * SEGS * CHUNKS, size)
+    row_grad = pl.pallas_call(
+        functools.partial(backward_kernel, experts=experts, rows=rows, at=cap % 8),
+        grid=(hidden_size // block,),
+        out_shape=shape_of(slots, width, dtype=bf16),
+        in_specs=[
+            whole(experts * SEGS * CHUNKS, size),
+            pl.BlockSpec((experts, 8, 128), lambda i: (0, cap // 8, 0)),
+            pre,
+            pre,
+            wide,
+            wide,
+            tall,
+        ],
+        out_specs=whole(slots, width),
+        scratch_shapes=[pltpu.VMEM((slots, width), f32)],
+        name="expert_backward",
+    )(grad_all, arrived, pre_gate, pre_up, gate_mat, up_mat, down_mat)
     back = exchange(row_grad.reshape(experts, rows, width), "expert").reshape(slots, width)
     gate_grad = pl.pallas_call(
         functools.partial(gate_grad_kernel, experts=experts, rows=rows),

time: 196 us -> 187 us (0.954)
  the two profiles are of different devices: /device:TPU:64 before, /device:TPU:1 now
where the time goes in v2:
time: 187 us; the launch traced here: 186 us
  blocking collectives  86.9 us (46%)
  Pallas kernels  38.1 us (20%)
  waiting for transfers between devices  35.2 us (19%)
  starting transfers between devices  21.9 us (12%)
  local copies, waits for them, and re-layouts  2.71 us (1%)
    all_to_all x5, blocking collectives, exchange(): return lax.all_to_all(values, axis, split_axis=0, concat_axis=0, tiled=True)  86.9 us
    all_to_all x3, waiting for transfers between devices, exchange(): return lax.all_to_all(values, axis, split_axis=0, concat_axis=0, tiled=True)  35.2 us
    all_to_all x3, starting transfers between devices, exchange(): return lax.all_to_all(values, axis, split_axis=0, concat_axis=0, tiled=True)  21.9 us
    pallas_call x1, Pallas kernels, shards(): pl.pallas_call(functools.partial(backward_kernel, experts=experts, rows=r...  10.4 us
    pallas_call x1, Pallas kernels, shards(): pl.pallas_call(forward_kernel, grid=(hidden_size // block,), out_shape=(s...  8.72 us
  transfers between devices with their start and end apart: 3, of which 3 were waited for; matrix products, arithmetic and copies ran while one was open for 0% of the time, Pallas kernels for 1%

profile of v2, /device:TPU:1, one launch (start us, length us, event | category | flops | bytes accessed | tf_op | source)
XLA Modules:
  0.0 186.1 jit_solution(12842569327934226338)
XLA Ops:
  0.6 3.3 %dispatch.1 = bf16[288,2048]{1,0:T(8,128)(2,1)} custom-call(bf16[128,2048]{1,0:T(8,128)(2,1)} %tok_ref.1, s32[2,128]{1,0:T(2,128)} %bitcast.38, bf16[2,128]{1,0:T(2,128)(2,1)} %bitcast.44), custom_call_target="tpu_custom_call" | custom-call | tf_op jit(solution)/shard_map/dispatch/pallas_call | solution.py:386
  3.9 15.4 %all_to_all.40.share_ref = bf16[4,72,2048]{2,1,0:T(8,128)(2,1)} all-to-all(bf16[4,72,2048]{2,1,0:T(8,128)(2,1)} %bitcast.30), channel_id=1, replica_groups=mesh['z'=12,'yc'=16,'expert'=4] {'expert'}, dimensions={0} | all-to-all | bytes 2359296 | tf_op jit(solution)/shard_map/all_to_all | solution.py:356
  19.3 8.7 %expert_forward.1 = (bf16[288,2048]{1,0:T(8,128)(2,1)}, f32[288,768]{1,0:T(8,128)}, f32[288,768]{1,0:T(8,128)}) custom-call(bf16[288,2048]{1,0:T(8,128)(2,1)} %bitcast.28, bf16[2048,768]{1,0:T(8,128)(2,1)} %bitcast.20, bf16[2048,768]{1,0:T(8,128)(2,1)} %bitcast.22, bf16[768,2048]{1,0:T(8,128)(2,1)} %bitcast.24), custom_call_target="tpu_custom_call" | custom-call | tf_op jit(solution)/shard_map/expert_forward/pallas_call | solution.py:400
  28.0 3.5 %all-to-all-start.1 = ((bf16[4,72,2048]{2,1,0:T(8,128)(2,1)}), bf16[4,72,2048]{2,1,0:T(8,128)(2,1)S(1)}, u32[]{:S(2)}, u32[]{:S(2)}) async-start(bf16[4,72,2048]{2,1,0:T(8,128)(2,1)} %bitcast.34), calls=%async_computation.1 | async-start | bytes 2359296 | tf_op jit(solution)/shard_map/all_to_all | solution.py:356
  32.2 9.8 %all-to-all-done.1 = bf16[4,72,2048]{2,1,0:T(8,128)(2,1)S(1)} async-done(((bf16[4,72,2048]{2,1,0:T(8,128)(2,1)}), bf16[4,72,2048]{2,1,0:T(8,128)(2,1)S(1)}, u32[]{:S(2)}, u32[]{:S(2)}) %all-to-all-start.1) | async-done | bytes 1179680 | tf_op jit(solution)/shard_map/all_to_all | solution.py:356
  41.9 0.0 copy-start
  41.9 1.0 copy-done
  43.0 2.9 %combine.1 = (bf16[128,2048]{1,0:T(8,128)(2,1)}, f32[24,256]{1,0:T(8,128)}, f32[24,128]{1,0:T(8,128)}, bf16[16,24,256]{2,1,0:T(8,128)(2,1)}, bf16[12,32,256]{2,1,0:T(8,128)(2,1)}) custom-call(bf16[288,2048]{1,0:T(8,128)(2,1)} %bitcast.26, s32[2,128]{1,0:T(2,128)} %bitcast.39, bf16[2,128]{1,0:T(2,128)(2,1)} %bitcast.45, bf16[1,2048]{1,0:T(2,128)(2,1)} %bitcast.42, ...), custom_call_target="tpu_custom_call" | custom-call | tf_op jit(solution)/shard_map/combine/pallas_call | solution.py:415
  45.9 29.8 %all_to_all.41 = bf16[16,24,256]{2,1,0:T(8,128)(2,1)} all-to-all(bf16[16,24,256]{2,1,0:T(8,128)(2,1)} %get-tuple-element.21), channel_id=1, replica_groups=mesh['z'=12,'yc'=16,'expert'=4] {'yc'}, dimensions={0} | all-to-all | bytes 393216 | tf_op jit(solution)/shard_map/all_to_all | solution.py:356
  75.6 14.9 %all-to-all-start.3 = ((bf16[12,32,256]{2,1,0:T(8,128)(2,1)}), bf16[12,32,256]{2,1,0:T(8,128)(2,1)S(1)}, u32[]{:S(2)}, u32[]{:S(2)}) async-start(bf16[12,32,256]{2,1,0:T(8,128)(2,1)} %get-tuple-element.22), calls=%async_computation.3 | async-start | bytes 393216 | tf_op jit(solution)/shard_map/all_to_all | solution.py:356
  90.5 13.0 %all-to-all-done.3 = bf16[12,32,256]{2,1,0:T(8,128)(2,1)S(1)} async-done(((bf16[12,32,256]{2,1,0:T(8,128)(2,1)}), bf16[12,32,256]{2,1,0:T(8,128)(2,1)S(1)}, u32[]{:S(2)}, u32[]{:S(2)}) %all-to-all-start.3) | async-done | bytes 196640 | tf_op jit(solution)/shard_map/all_to_all | solution.py:356
  103.5 0.0 copy-start.2
  103.5 0.7 copy-done.2
  104.2 3.4 %score.1 = (bf16[16,32,256]{2,1,0:T(8,128)(2,1)}, f32[3,16,128]{2,1,0:T(8,128)}) custom-call(bf16[384,256]{1,0:T(8,128)(2,1)} %bitcast.32, bf16[384,256]{1,0:T(8,128)(2,1)} %bitcast.35, s32[1,1]{1,0:T(1,128)} %bitcast.13.me_ref), custom_call_target="tpu_custom_call" | custom-call | tf_op jit(solution)/shard_map/score/pallas_call | solution.py:430
  107.7 17.8 %all_to_all.42.got_ref = bf16[16,32,256]{2,1,0:T(8,128)(2,1)} all-to-all(bf16[16,32,256]{2,1,0:T(8,128)(2,1)} %get-tuple-element.23), channel_id=1, replica_groups=mesh['z'=12,'yc'=16,'expert'=4] {'yc'}, dimensions={0} | all-to-all | bytes 524288 | tf_op jit(solution)/shard_map/all_to_all | solution.py:356
  125.5 2.3 %coeff.1 = (f32[8,256]{1,0:T(8,128)}, bf16[192,256]{1,0:T(8,128)(2,1)}, f32[1,128]{1,0:T(1,128)}) custom-call(bf16[16,32,256]{2,1,0:T(8,128)(2,1)} %all_to_all.42.got_ref, f32[3,16,128]{2,1,0:T(8,128)} %get-tuple-element.24.saved_ref, bf16[384,256]{1,0:T(8,128)(2,1)} %bitcast.33, s32[1,1]{1,0:T(1,128)} %bitcast.13.me_ref), custom_call_target="tpu_custom_call" | custom-call | tf_op jit(solution)/shard_map/coeff/pallas_call | solution.py:438
  127.8 15.2 %all_to_all.43.dp_ref = bf16[12,16,256]{2,1,0:T(8,128)(2,1)} all-to-all(bf16[12,16,256]{2,1,0:T(8,128)(2,1)} %bitcast.37), channel_id=1, replica_groups=mesh['z'=12,'yc'=16,'expert'=4] {'z'}, dimensions={0} | all-to-all | bytes 196608 | tf_op jit(solution)/shard_map/all_to_all | solution.py:356
  143.0 1.7 text_grad.1
  144.7 8.6 %all_to_all.44 = f32[4,24,256]{2,1,0:T(8,128)} all-to-all(f32[4,24,256]{2,1,0:T(8,128)} %get-tuple-element.29), channel_id=1, replica_groups=mesh['z'=12,'yc'=16,'expert'=4] {'expert'}, dimensions={0} | all-to-all | bytes 196608 | tf_op jit(solution)/shard_map/all_to_all | solution.py:356
  153.3 10.4 %expert_backward.1 = bf16[288,2048]{1,0:T(8,128)(2,1)} custom-call(f32[96,256]{1,0:T(8,128)} %bitcast.36, bf16[4,72,2048]{2,1,0:T(8,128)(2,1)} %all_to_all.40.share_ref, f32[288,768]{1,0:T(8,128)} %get-tuple-element.30.pre_gate_ref, f32[288,768]{1,0:T(8,128)} %get-tuple-element.31.pre_up_ref, bf16[2048,768]{1,0:T(8,128)(2,1)} %bitcast.21, ...), custom_call_target="tpu_custom_call" | custom-call | tf_op jit(solution)/shard_map/expert_backward/pallas_call | solution.py:454
  163.7 3.5 %all-to-all-start.7 = ((bf16[4,72,2048]{2,1,0:T(8,128)(2,1)}), bf16[4,72,2048]{2,1,0:T(8,128)(2,1)S(1)}, u32[]{:S(2)}, u32[]{:S(2)}) async-start(bf16[4,72,2048]{2,1,0:T(8,128)(2,1)} %bitcast.31), calls=%async_computation.7 | async-start | bytes 2359296 | tf_op jit(solution)/shard_map/all_to_all | solution.py:356
  167.2 2.7 %gate_grad.1 = f32[2,128]{1,0:T(2,128)} custom-call(bf16[288,2048]{1,0:T(8,128)(2,1)} %bitcast.27, s32[2,128]{1,0:T(2,128)} %bitcast.40, f32[24,256]{1,0:T(8,128)} %get-tuple-element.32.grad_ref), custom_call_target="tpu_custom_call" | custom-call | tf_op jit(solution)/shard_map/gate_grad/pallas_call | solution.py:472
  170.0 12.4 %all-to-all-done.7 = bf16[4,72,2048]{2,1,0:T(8,128)(2,1)S(1)} async-done(((bf16[4,72,2048]{2,1,0:T(8,128)(2,1)}), bf16[4,72,2048]{2,1,0:T(8,128)(2,1)S(1)}, u32[]{:S(2)}, u32[]{:S(2)}) %all-to-all-start.7) | async-done | bytes 1179680 | tf_op jit(solution)/shard_map/all_to_all | solution.py:356
  182.4 0.0 copy-start.1
  182.4 1.0 copy-done.1
  183.4 2.7 %token_grad.1 = bf16[128,2048]{1,0:T(8,128)(2,1)} custom-call(bf16[288,2048]{1,0:T(8,128)(2,1)} %bitcast.29, s32[2,128]{1,0:T(2,128)} %bitcast.41), custom_call_target="tpu_custom_call" | custom-call | tf_op jit(solution)/shard_map/token_grad/pallas_call | solution.py:479
Async XLA Ops:
  28.0 13.9 %all-to-all-start.1 = ((bf16[4,72,2048]{2,1,0:T(8,128)(2,1)}), bf16[4,72,2048]{2,1,0:T(8,128)(2,1)S(1)}, u32[]{:S(2)}, u32[]{:S(2)}) async-start(bf16[4,72,2048]{2,1,0:T(8,128)(2,1)} %bitcast.34), calls=%async_computation.1 | async-start | bytes 2359296 | tf_op jit(solution)/shard_map/all_to_all | solution.py:356
  41.9 1.0 copy-start
  75.6 27.9 %all-to-all-start.3 = ((bf16[12,32,256]{2,1,0:T(8,128)(2,1)}), bf16[12,32,256]{2,1,0:T(8,128)(2,1)S(1)}, u32[]{:S(2)}, u32[]{:S(2)}) async-start(bf16[12,32,256]{2,1,0:T(8,128)(2,1)} %get-tuple-element.22), calls=%async_computation.3 | async-start | bytes 393216 | tf_op jit(solution)/shard_map/all_to_all | solution.py:356
  103.5 0.7 copy-start.2
  163.7 18.7 %all-to-all-start.7 = ((bf16[4,72,2048]{2,1,0:T(8,128)(2,1)}), bf16[4,72,2048]{2,1,0:T(8,128)(2,1)S(1)}, u32[]{:S(2)}, u32[]{:S(2)}) async-start(bf16[4,72,2048]{2,1,0:T(8,128)(2,1)} %bitcast.31), calls=%async_computation.7 | async-start | bytes 2359296 | tf_op jit(solution)/shard_map/all_to_all | solution.py:356
  182.4 1.0 copy-start.1
